TPU v7x, 512 devices: a whole 4x4x16 slice. The times are simulated.
512 devices in a mesh: prow: 16 (over x, y), pcol: 32 (over z, core).
Axes of the slice: x: 4, y: 4, z: 16, core: 2. Of those that a mesh axis runs over, the one named last changes fastest.
Arguments:
- adjoint_trail: float32 [2, 16, 256, 1, 32, 256], P(None, 'prow', None, None, 'pcol'), as said below
- factor_low: float32 [2, 16, 32, 8, 4, 256], P(None, 'prow', 'pcol'), may hold values from -0.0625 to 0.0625
- adjoint_low: float32 [2, 16, 32, 8, 4, 256], P(None, 'prow', 'pcol'), may hold values from -6 to 6
- factor_top: float32 [10, 256, 256], P(None, 'pcol'), as said below
- adjoint_top: float32 [10, 256, 256], P(None, 'pcol'), may hold values from -6 to 6
- diag_inverse: float32 [4, 256, 256], P(None, 'pcol'), as said below
Outputs:
- grad_low: float32 [2, 16, 32, 8, 4, 256], P(None, 'prow', 'pcol')
- grad_top: float32 [10, 256, 256], P(None, 'pcol')
Inputs may be any that keep to these rules, and one draw needn't show every extreme that they name: adjoint_trail reshaped row-major to 8192 x 8192 is symmetric. The diagonal blocks factor_top[j (j + 1) / 2 + j] are lower triangular with a positive diagonal. diag_inverse[j] is the inverse of factor_top[j (j + 1) / 2 + j].
All inputs are finite; a program needn't handle non-finite values.
Results may differ from a plain program's by a relative error of at most 0.00024.
Values sent between devices are 32-bit elements; how exact they have to be, the bound alone decides.
A program may use at most 64 MiB of HBM per device.

v0:
```python
import jax
import jax.numpy as jnp
from jax import lax
from jax.sharding import PartitionSpec as P

NB = 256
K = 4
HIGHEST = lax.Precision.HIGHEST


def from_root(array, axis, root):
    mine = lax.axis_index(axis) == root
    return lax.psum(jnp.where(mine, array, jnp.zeros_like(array)), axis)


def matmul(left, right):
    return jnp.dot(left, right, precision=HIGHEST, preferred_element_type=jnp.float32)


def inner_product(left, right):
    return lax.dot_general(
        left, right, (((0,), (0,)), ((), ())), precision=HIGHEST, preferred_element_type=jnp.float32
    )


def block_slot(row_block, col_block):
    return row_block * (row_block + 1) // 2 + col_block


def half_lower(square):
    size = square.shape[0]
    row_ids = lax.broadcasted_iota(jnp.int32, (size, size), 0)
    col_ids = lax.broadcasted_iota(jnp.int32, (size, size), 1)
    return jnp.where(row_ids > col_ids, square, jnp.where(row_ids == col_ids, 0.5 * square, 0.0))


def diagonal_adjoint(diagonal, inverse, lower_adj):
    inner = half_lower(inner_product(jnp.tril(diagonal), lower_adj))
    spread = inner_product(inverse, matmul(inner, inverse))
    return 0.5 * (spread + spread.T)


def rows_one(piece):
    return lax.all_gather(piece, "pcol", axis=1, tiled=True)


def owner_one(piece, root):
    return from_root(piece, "prow", root)


def reduce_one(term, count):
    return lax.psum_scatter(
        term(jnp.int32(0), lax.axis_size("pcol") * count), "pcol", scatter_dimension=0, tiled=True
    )


def trailing_product(trail, panels, gather_rows, send_owner, reduce_rows):
    prow_count = lax.axis_size("prow")
    pcol_count = lax.axis_size("pcol")
    cycles, sub_rows, width = panels.shape
    block = sub_rows * pcol_count
    gathered = gather_rows(panels[:, None]).reshape(cycles, block, width)
    column = lax.axis_index("pcol")
    col_cycles = trail.shape[3]
    global_block = 0 + column
    share = lax.dynamic_index_in_dim(gathered, global_block // prow_count, 0, keepdims=False)
    owned = [send_owner(share, global_block % prow_count)]
    stacked = jnp.stack(owned)
    view = trail.reshape(cycles, pcol_count, sub_rows, col_cycles, block)
    unit = cycles * sub_rows

    def term(start, count):
        product = jnp.einsum(
            "iaekb,kbn->aien", view, stacked, precision=HIGHEST, preferred_element_type=jnp.float32
        )
        return product.reshape(count, width)

    return reduce_rows(term, unit).reshape(cycles, sub_rows, width)


def per_device(adjoint_trail, factor_low, adjoint_low, factor_top, adjoint_top, diag_inverse):
    cycles = factor_low.shape[0]
    sub_rows = factor_low.shape[3]
    local_rows = cycles * sub_rows
    low_factor = factor_low.reshape(cycles, sub_rows, K * NB)
    low_adjoint = adjoint_low.reshape(local_rows, K, NB)
    columns = low_factor.reshape(local_rows, K, NB)
    top_factor, top_adjoint, inverses = (
        lax.all_gather(factor_top, "pcol", axis=1, tiled=True),
        lax.all_gather(adjoint_top, "pcol", axis=1, tiled=True),
        lax.all_gather(diag_inverse, "pcol", axis=1, tiled=True),
    )
    lower_grads = [None] * K
    diag_grads = [None] * K
    upper_grads = {}
    grams = {}

    def lower_step(panel):
        single = low_factor[:, :, panel * NB : (panel + 1) * NB]
        image = trailing_product(adjoint_trail, single, rows_one, owner_one, reduce_one).reshape(
            local_rows, NB
        )
        residual = low_adjoint[:, panel] - 2.0 * image
        for later in range(panel + 1, K):
            residual = residual - matmul(lower_grads[later], top_factor[block_slot(later, panel)])
        lower_grads[panel] = matmul(residual, inverses[panel])

    def top_step(panel):
        for row_block in range(panel + 1, K):
            top_residual = top_adjoint[block_slot(row_block, panel)] - grams[row_block, panel]
            top_residual = top_residual - 2.0 * matmul(
                diag_grads[row_block], top_factor[block_slot(row_block, panel)]
            )
            for middle in range(panel + 1, row_block):
                top_residual = top_residual - matmul(
                    upper_grads[middle, row_block], top_factor[block_slot(middle, panel)]
                )
            for beyond in range(row_block + 1, K):
                top_residual = top_residual - inner_product(
                    upper_grads[row_block, beyond], top_factor[block_slot(beyond, panel)]
                )
            upper_grads[panel, row_block] = matmul(top_residual, inverses[panel])
        lower_adj = top_adjoint[block_slot(panel, panel)] - grams[panel, panel]
        for row_block in range(panel + 1, K):
            lower_adj = lower_adj - inner_product(
                upper_grads[panel, row_block], top_factor[block_slot(row_block, panel)]
            )
        diag_grads[panel] = diagonal_adjoint(
            top_factor[block_slot(panel, panel)], inverses[panel], jnp.tril(lower_adj)
        )

    for panel in reversed(range(K)):
        lower_step(panel)
        local_gram = jnp.stack(
            [inner_product(lower_grads[panel], columns[:, earlier]) for earlier in range(panel + 1)]
        )
        summed = lax.psum(local_gram, ("prow", "pcol"))
        for earlier in range(panel + 1):
            grams[panel, earlier] = summed[earlier]
        top_step(panel)
    grad_low = jnp.stack(lower_grads, 1).reshape(factor_low.shape)
    blocks = []
    for row_block in range(K):
        for col_block in range(row_block + 1):
            if row_block == col_block:
                blocks.append(diag_grads[col_block])
            else:
                blocks.append(upper_grads[col_block, row_block])
    full_top = jnp.stack(blocks)
    share_rows = factor_top.shape[1]
    grad_top = lax.dynamic_slice_in_dim(
        full_top, lax.axis_index("pcol") * share_rows, share_rows, 1
    )
    return (grad_low, grad_top)


def solution(mesh):
    in_specs = (
        P(None, "prow", None, None, "pcol", None),
        P(None, "prow", "pcol", None, None, None),
        P(None, "prow", "pcol", None, None, None),
        P(None, "pcol", None),
        P(None, "pcol", None),
        P(None, "pcol", None),
    )
    out_specs = (P(None, "prow", "pcol", None, None, None), P(None, "pcol", None))
    return jax.shard_map(
        per_device, mesh=mesh, in_specs=in_specs, out_specs=out_specs, check_vma=False
    )
```

profile of v0, /device:TPU:8, one launch (start us, length us, event | category | flops | bytes accessed | tf_op | source)
XLA Modules:
  0.0 1294.8 jit_solution(6312719842912323253)
XLA Ops:
  9.0 37.8 %all-gather.3 = f32[2,256,256]{2,1,0:T(8,128)S(1)} all-gather(f32[2,8,256]{2,1,0:T(8,128)S(1)} %get-tuple-element.15), channel_id=5, replica_groups=mesh['prow'=16,'pcol'=32] {'pcol'}, dimensions={1}, use_global_device_ids=true | all-gather | bytes 540672 | tf_op jit(solution)/shard_map/all_gather | solution.py:44
  46.8 28.5 %all-gather.2 = f32[2,256,256]{2,1,0:T(8,128)S(1)} all-gather(f32[2,8,256]{2,1,0:T(8,128)S(1)} %get-tuple-element.16), channel_id=4, replica_groups=mesh['prow'=16,'pcol'=32] {'pcol'}, dimensions={1}, use_global_device_ids=true | all-gather | bytes 540672 | tf_op jit(solution)/shard_map/all_gather | solution.py:44
  76.7 29.8 %all-gather.1 = f32[2,256,256]{2,1,0:T(8,128)S(1)} all-gather(f32[2,8,256]{2,1,0:T(8,128)S(1)} %get-tuple-element.17), channel_id=3, replica_groups=mesh['prow'=16,'pcol'=32] {'pcol'}, dimensions={1}, use_global_device_ids=true | all-gather | bytes 540672 | tf_op jit(solution)/shard_map/all_gather | solution.py:44
  107.3 28.5 %all-gather = f32[2,256,256]{2,1,0:T(8,128)S(1)} all-gather(f32[2,8,256]{2,1,0:T(8,128)S(1)} %get-tuple-element.14), channel_id=2, replica_groups=mesh['prow'=16,'pcol'=32] {'pcol'}, dimensions={1}, use_global_device_ids=true | all-gather | bytes 540672 | tf_op jit(solution)/shard_map/all_gather | solution.py:44
  137.2 113.6 %all-reduce.7.cloned.1.call-done = (f32[256,256]{1,0:T(8,128)}, f32[256,256]{1,0:T(8,128)}, f32[256,256]{1,0:T(8,128)}, f32[256,256]{1,0:T(8,128)}) async-done(((f32[256,256]{1,0:T(8,128)}, f32[256,256]{1,0:T(8,128)}, f32[256,256]{1,0:T(8,128)}, f32[256,256]{1,0:T(8,128)}), (f32[256,256]{1,0:T(8,128)}, f32[256,256]{1,0:T(8,128)}, f32[256,256]{1,0:T(8,128)}, ...) | async-done | bytes 1048592 | tf_op jit(solution)/shard_map/psum | solution.py:13
  250.9 1.7 convolution_bitcast_fusion
  261.1 99.8 %reduce-scatter.11.cloned.1.call-done = f32[16,256]{1,0:T(8,128)} async-done(((f32[512,256]{1,0:T(8,128)}), f32[16,256]{1,0:T(8,128)}) %reduce-scatter.11.cloned.1.call-update) | async-done | bytes 16400 | tf_op jit(solution)/shard_map/reduce_scatter | solution.py:52
  364.8 104.2 %reduce-scatter.9.cloned.1.call-done = f32[16,256]{1,0:T(8,128)} async-done(((f32[512,256]{1,0:T(8,128)}), f32[16,256]{1,0:T(8,128)}) %reduce-scatter.9.cloned.1.call-update) | async-done | bytes 16400 | tf_op jit(solution)/shard_map/reduce_scatter | solution.py:52
  469.0 72.4 %all-gather.10.cloned.1.call-done = f32[10,256,256]{2,1,0:T(8,128)} async-done(((f32[10,8,256]{2,1,0:T(8,128)}), f32[10,256,256]{2,1,0:T(8,128)}) %all-gather.10.cloned.1.call-update) | async-done | bytes 2621456 | tf_op jit(solution)/shard_map/all_gather | solution.py:89
  541.4 1.3 convolution_subtract_fusion.19
  545.2 103.2 %reduce-scatter.7.cloned.1.call-done = f32[16,256]{1,0:T(8,128)} async-done(((f32[512,256]{1,0:T(8,128)}), f32[16,256]{1,0:T(8,128)}) %reduce-scatter.7.cloned.1.call-update) | async-done | bytes 16400 | tf_op jit(solution)/shard_map/reduce_scatter | solution.py:52
  648.4 1.2 convolution_subtract_fusion.18
  654.2 102.5 %reduce-scatter.5.cloned.1.call-done = f32[16,256]{1,0:T(8,128)} async-done(((f32[512,256]{1,0:T(8,128)}), f32[16,256]{1,0:T(8,128)}) %reduce-scatter.5.cloned.1.call-update) | async-done | bytes 16400 | tf_op jit(solution)/shard_map/reduce_scatter | solution.py:52
  760.5 1.9 pad_maximum_fusion.2
  764.3 65.2 %all-gather.12.cloned.1.call-done = f32[10,256,256]{2,1,0:T(8,128)} async-done(((f32[10,8,256]{2,1,0:T(8,128)}), f32[10,256,256]{2,1,0:T(8,128)}) %all-gather.12.cloned.1.call-update) | async-done | bytes 2621456 | tf_op jit(solution)/shard_map/all_gather | solution.py:90
  829.5 417.1 %all-reduce.5.cloned.1.call-done = (f32[2,256,256]{2,1,0:T(8,128)}, f32[3,256,256]{2,1,0:T(8,128)}, f32[4,256,256]{2,1,0:T(8,128)}, f32[1,256,256]{2,1,0:T(8,128)}) async-done(((f32[2,256,256]{2,1,0:T(8,128)}, f32[3,256,256]{2,1,0:T(8,128)}, f32[4,256,256]{2,1,0:T(8,128)}, f32[1,256,256]{2,1,0:T(8,128)}), (f32[2,256,256]{2,1,0:T(8,128)}, f32[3,256,256]{2,1,0:T(8,128)}, f32[4,256,256]{2,1,0:T(8,128)}, ...) | async-done | bytes 2621456 | tf_op jit(solution)/shard_map/psum | solution.py:137
  1246.6 1.5 fusion.18
  1248.1 1.3 fusion.62
  1249.5 1.5 fusion.66
  1251.2 1.5 fusion.8
  1252.7 1.3 fusion.69
  1254.0 1.6 fusion.7
  1258.0 1.5 fusion.5
  1260.0 1.3 fusion.72
  1261.3 1.5 fusion.6
  1264.8 1.6 convolution_subtract_fusion.11
  1267.9 1.3 fusion.71
  1269.2 1.8 copy.38
  1271.0 1.5 fusion.1
  1272.5 1.5 fusion.2
  1276.7 1.4 fusion.3
  1279.8 1.6 convolution_subtract_fusion.6
  (154 shorter events, 45.4 us)
Async XLA Ops:
  8.0 242.9 %all-reduce.7.cloned.1.call-start = ((), (), s32[]{:S(2)}) async-start(), calls=%async_computation.12 | async-start | bytes 2097152 | tf_op jit(solution)/shard_map/psum | solution.py:13
  9.0 128.2 %copy-start.19 = (f32[2,1,256,1,1,256]{5,4,3,2,1,0:T(1,128)S(1)}, f32[2,1,256,1,1,256]{5,4,3,2,1,0:T(1,128)}, u32[]{:S(2)}) copy-start(f32[2,1,256,1,1,256]{5,4,3,2,1,0:T(1,128)} %param.6) | copy-start | bytes 1572868
  136.6 124.5 %all-gather.8.cloned.1.call-start = ((), (), s32[]{:S(2)}) async-start(), calls=%async_computation.8 | async-start | bytes 1081344 | tf_op jit(solution)/shard_map/all_gather | solution.py:91
  137.1 223.8 %reduce-scatter.11.cloned.1.call-start = ((), (), s32[]{:S(2)}) async-start(), calls=%async_computation.7 | async-start | bytes 540672 | tf_op jit(solution)/shard_map/reduce_scatter | solution.py:52
  250.8 2.9 copy-start.25
  250.9 5.5 copy-start.24
  253.7 215.4 %reduce-scatter.9.cloned.1.call-start = ((), (), s32[]{:S(2)}) async-start(), calls=%async_computation.6 | async-start | bytes 540672 | tf_op jit(solution)/shard_map/reduce_scatter | solution.py:52
  253.7 4.6 copy-start.23
  255.6 285.9 %all-gather.10.cloned.1.call-start = ((), (), s32[]{:S(2)}) async-start(), calls=%async_computation.9 | async-start | bytes 2703360 | tf_op jit(solution)/shard_map/all_gather | solution.py:89
  256.3 392.1 %reduce-scatter.7.cloned.1.call-start = ((), (), s32[]{:S(2)}) async-start(), calls=%async_computation.5 | async-start | bytes 540672 | tf_op jit(solution)/shard_map/reduce_scatter | solution.py:52
  256.4 4.6 copy-start.27
  257.0 3.9 copy-start.26
  258.2 498.6 %reduce-scatter.5.cloned.1.call-start = ((), (), s32[]{:S(2)}) async-start(), calls=%async_computation.4 | async-start | bytes 540672 | tf_op jit(solution)/shard_map/reduce_scatter | solution.py:52
  260.1 569.4 %all-gather.12.cloned.1.call-start = ((), (), s32[]{:S(2)}) async-start(), calls=%async_computation.10 | async-start | bytes 2703360 | tf_op jit(solution)/shard_map/all_gather | solution.py:90
  260.7 985.9 %all-reduce.5.cloned.1.call-start = ((), (), s32[]{:S(2)}) async-start(), calls=%async_computation.11 | async-start | bytes 5242880 | tf_op jit(solution)/shard_map/psum | solution.py:137
  541.4 215.3 %copy-start = (f32[10,256,256]{2,1,0:T(8,128)S(1)}, f32[10,256,256]{2,1,0:T(8,128)}, u32[]{:S(2)}) copy-start(f32[10,256,256]{2,1,0:T(8,128)} %all-gather.10.cloned.1.call-done) | copy-start | bytes 7864324
  1251.1 5.0 copy-start.1
  1258.0 3.3 copy-start.11
  1258.0 5.4 copy-start.2
  1259.6 5.2 copy-start.20
  1261.3 5.7 copy-start.7
  1271.0 3.1 copy-start.8
  1271.0 3.9 copy-start.3
  1271.0 4.3 copy-start.5
  1275.2 6.8 copy-start.14
  1276.2 3.5 copy-start.22
  1276.7 4.7 copy-start.17
  1279.7 3.9 copy-start.13
  1283.2 3.3 copy-start.18
  1283.2 3.3 copy-start.6
  1283.2 3.3 copy-start.12
  1283.6 3.0 copy-start.15
  (5 other events, 9.8 us)
Sparse Core Ops, SparseCore 0:
  136.7 114.1 all-reduce.6
  763.6 482.9 all-reduce.4
Sparse Core Ops, SparseCore 1:
  139.2 67.6 all-gather.7
  253.7 107.1 reduce-scatter.10
  363.8 105.2 reduce-scatter.8
  471.2 70.2 all-gather.9
  544.2 104.1 reduce-scatter.6
  651.4 105.3 reduce-scatter.4
  758.8 70.6 all-gather.11
where the time goes:
time: 1300 us; the launch traced here: 1290 us
  waiting for transfers between devices  1080 us (83%)
  blocking collectives  125 us (10%)
  matrix products  53.2 us (4%)
  between operations  16.7 us (1%)
    psum x1, waiting for transfers between devices, per_device(): summed = lax.psum(local_gram, ('prow', 'pcol'))  417 us
    reduce_scatter x4, waiting for transfers between devices, reduce_one(): lax.psum_scatter(term(jnp.int32(0), lax.axis_size('pcol') * count), 'pcol...  410 us
    all_gather x4, blocking collectives, rows_one(): return lax.all_gather(piece, 'pcol', axis=1, tiled=True)  125 us
    psum x1, waiting for transfers between devices, from_root(): return lax.psum(jnp.where(mine, array, jnp.zeros_like(array)), axis)  114 us
    all_gather x1, waiting for transfers between devices, per_device(): lax.all_gather(factor_top, 'pcol', axis=1, tiled=True)  72.4 us
    all_gather x1, waiting for transfers between devices, per_device(): lax.all_gather(adjoint_top, 'pcol', axis=1, tiled=True)  65.2 us
    dot_general x30, matrix products, matmul(): jnp.dot(left, right, precision=HIGHEST, preferred_element_type=jnp.float32)  27.1 us
  transfers between devices with their start and end apart: 9, of which 8 were waited for; matrix products, arithmetic and copies ran while one was open for 2% of the time, Pallas kernels for 0%

commit v1 on v0

--- a/solution.py
+++ b/solution.py
@@ -134,7 +134,7 @@
         local_gram = jnp.stack(
             [inner_product(lower_grads[panel], columns[:, earlier]) for earlier in range(panel + 1)]
         )
-        summed = lax.psum(local_gram, ("prow", "pcol"))
+        summed = lax.psum(lax.psum(local_gram, "prow"), "pcol")
         for earlier in range(panel + 1):
             grams[panel, earlier] = summed[earlier]
         top_step(panel)

time: 1300 us -> 1150 us (0.88)
  the two profiles are of different devices: /device:TPU:8 before, /device:TPU:1 now
where the time goes in v1:
time: 1150 us
  waiting for transfers between devices  934 us (81%)
  blocking collectives  126 us (11%)
  matrix products  53.2 us (5%)
  between operations  16.7 us (1%)
    reduce_scatter x4, waiting for transfers between devices, reduce_one(): lax.psum_scatter(term(jnp.int32(0), lax.axis_size('pcol') * count), 'pcol...  405 us
    psum x2, waiting for transfers between devices, per_device(): summed = lax.psum(lax.psum(local_gram, 'prow'), 'pcol')  339 us
    all_gather x4, blocking collectives, rows_one(): return lax.all_gather(piece, 'pcol', axis=1, tiled=True)  126 us
    psum x1, waiting for transfers between devices, from_root(): return lax.psum(jnp.where(mine, array, jnp.zeros_like(array)), axis)  112 us
    all_gather x1, waiting for transfers between devices, per_device(): lax.all_gather(factor_top, 'pcol', axis=1, tiled=True)  76.1 us
    dot_general x30, matrix products, matmul(): jnp.dot(left, right, precision=HIGHEST, preferred_element_type=jnp.float32)  27.1 us
  transfers between devices with their start and end apart: 10, of which 8 were waited for; matrix products, arithmetic and copies ran while one was open for 2% of the time, Pallas kernels for 0%

profile of v1, /device:TPU:1, one launch (start us, length us, event | category | flops | bytes accessed | tf_op | source)
XLA Modules:
  0.0 1150.2 jit_solution(7169482205904475710)
XLA Ops:
  9.0 39.1 %all-gather.3 = f32[2,256,256]{2,1,0:T(8,128)S(1)} all-gather(f32[2,8,256]{2,1,0:T(8,128)S(1)} %get-tuple-element.19), channel_id=5, replica_groups=mesh['prow'=16,'pcol'=32] {'pcol'}, dimensions={1}, use_global_device_ids=true | all-gather | bytes 540672 | tf_op jit(solution)/shard_map/all_gather | solution.py:44
  48.1 28.5 %all-gather.2 = f32[2,256,256]{2,1,0:T(8,128)S(1)} all-gather(f32[2,8,256]{2,1,0:T(8,128)S(1)} %get-tuple-element.20), channel_id=4, replica_groups=mesh['prow'=16,'pcol'=32] {'pcol'}, dimensions={1}, use_global_device_ids=true | all-gather | bytes 540672 | tf_op jit(solution)/shard_map/all_gather | solution.py:44
  78.1 29.8 %all-gather.1 = f32[2,256,256]{2,1,0:T(8,128)S(1)} all-gather(f32[2,8,256]{2,1,0:T(8,128)S(1)} %get-tuple-element.21), channel_id=3, replica_groups=mesh['prow'=16,'pcol'=32] {'pcol'}, dimensions={1}, use_global_device_ids=true | all-gather | bytes 540672 | tf_op jit(solution)/shard_map/all_gather | solution.py:44
  108.6 28.5 %all-gather = f32[2,256,256]{2,1,0:T(8,128)S(1)} all-gather(f32[2,8,256]{2,1,0:T(8,128)S(1)} %get-tuple-element.18), channel_id=2, replica_groups=mesh['prow'=16,'pcol'=32] {'pcol'}, dimensions={1}, use_global_device_ids=true | all-gather | bytes 540672 | tf_op jit(solution)/shard_map/all_gather | solution.py:44
  138.5 112.3 %all-reduce.11.cloned.1.call-done = (f32[256,256]{1,0:T(8,128)}, f32[256,256]{1,0:T(8,128)}, f32[256,256]{1,0:T(8,128)}, f32[256,256]{1,0:T(8,128)}) async-done(((f32[256,256]{1,0:T(8,128)}, f32[256,256]{1,0:T(8,128)}, f32[256,256]{1,0:T(8,128)}, f32[256,256]{1,0:T(8,128)}), (f32[256,256]{1,0:T(8,128)}, f32[256,256]{1,0:T(8,128)}, f32[256,256]{1,0:T(8,128)}, ...) | async-done | bytes 1048592 | tf_op jit(solution)/shard_map/psum | solution.py:13
  250.8 1.7 convolution_bitcast_fusion
  260.2 98.6 %reduce-scatter.11.cloned.1.call-done = f32[16,256]{1,0:T(8,128)} async-done(((f32[512,256]{1,0:T(8,128)}), f32[16,256]{1,0:T(8,128)}) %reduce-scatter.11.cloned.1.call-update) | async-done | bytes 16400 | tf_op jit(solution)/shard_map/reduce_scatter | solution.py:52
  362.7 104.0 %reduce-scatter.9.cloned.1.call-done = f32[16,256]{1,0:T(8,128)} async-done(((f32[512,256]{1,0:T(8,128)}), f32[16,256]{1,0:T(8,128)}) %reduce-scatter.9.cloned.1.call-update) | async-done | bytes 16400 | tf_op jit(solution)/shard_map/reduce_scatter | solution.py:52
  466.7 76.1 %all-gather.10.cloned.1.call-done = f32[10,256,256]{2,1,0:T(8,128)} async-done(((f32[10,8,256]{2,1,0:T(8,128)}), f32[10,256,256]{2,1,0:T(8,128)}) %all-gather.10.cloned.1.call-update) | async-done | bytes 2621456 | tf_op jit(solution)/shard_map/all_gather | solution.py:89
  542.7 1.3 convolution_subtract_fusion.19
  546.5 100.2 %reduce-scatter.7.cloned.1.call-done = f32[16,256]{1,0:T(8,128)} async-done(((f32[512,256]{1,0:T(8,128)}), f32[16,256]{1,0:T(8,128)}) %reduce-scatter.7.cloned.1.call-update) | async-done | bytes 16400 | tf_op jit(solution)/shard_map/reduce_scatter | solution.py:52
  646.7 1.2 convolution_subtract_fusion.18
  652.5 102.3 %reduce-scatter.5.cloned.1.call-done = f32[16,256]{1,0:T(8,128)} async-done(((f32[512,256]{1,0:T(8,128)}), f32[16,256]{1,0:T(8,128)}) %reduce-scatter.5.cloned.1.call-update) | async-done | bytes 16400 | tf_op jit(solution)/shard_map/reduce_scatter | solution.py:52
  758.6 1.9 pad_maximum_fusion.2
  762.3 123.3 %all-reduce.9.cloned.1.call-done = (f32[2,256,256]{2,1,0:T(8,128)}, f32[3,256,256]{2,1,0:T(8,128)}, f32[4,256,256]{2,1,0:T(8,128)}, f32[1,256,256]{2,1,0:T(8,128)}) async-done(((f32[2,256,256]{2,1,0:T(8,128)}, f32[3,256,256]{2,1,0:T(8,128)}, f32[4,256,256]{2,1,0:T(8,128)}, f32[1,256,256]{2,1,0:T(8,128)}), (f32[2,256,256]{2,1,0:T(8,128)}, f32[3,256,256]{2,1,0:T(8,128)}, f32[4,256,256]{2,1,0:T(8,128)}, ...) | async-done | bytes 2621456 | tf_op jit(solution)/shard_map/psum | solution.py:137
  886.4 215.6 %all-reduce.7.cloned.1.call-done = (f32[2,256,256]{2,1,0:T(8,128)}, f32[3,256,256]{2,1,0:T(8,128)}, f32[4,256,256]{2,1,0:T(8,128)}, f32[1,256,256]{2,1,0:T(8,128)}) async-done(((f32[2,256,256]{2,1,0:T(8,128)}, f32[3,256,256]{2,1,0:T(8,128)}, f32[4,256,256]{2,1,0:T(8,128)}, f32[1,256,256]{2,1,0:T(8,128)}), (f32[2,256,256]{2,1,0:T(8,128)}, f32[3,256,256]{2,1,0:T(8,128)}, f32[4,256,256]{2,1,0:T(8,128)}, ...) | async-done | bytes 2621456 | tf_op jit(solution)/shard_map/psum | solution.py:137
  1102.0 1.5 fusion.18
  1103.5 1.3 fusion.62
  1104.8 1.5 fusion.66
  1106.6 1.5 fusion.8
  1108.1 1.3 fusion.69
  1109.4 1.6 fusion.7
  1113.4 1.5 fusion.5
  1115.3 1.3 fusion.72
  1116.7 1.5 fusion.6
  1119.9 1.6 convolution_subtract_fusion.11
  1123.0 1.3 fusion.71
  1124.4 1.8 copy.38
  1126.2 1.5 fusion.1
  1127.7 1.5 fusion.2
  1132.1 1.4 fusion.3
  1135.2 1.6 convolution_subtract_fusion.6
  (157 shorter events, 45.2 us)
Async XLA Ops:
  8.0 242.8 %all-reduce.11.cloned.1.call-start = ((), (), s32[]{:S(2)}) async-start(), calls=%async_computation.13 | async-start | bytes 2097152 | tf_op jit(solution)/shard_map/psum | solution.py:13
  9.0 129.5 %copy-start.19 = (f32[2,1,256,1,1,256]{5,4,3,2,1,0:T(1,128)S(1)}, f32[2,1,256,1,1,256]{5,4,3,2,1,0:T(1,128)}, u32[]{:S(2)}) copy-start(f32[2,1,256,1,1,256]{5,4,3,2,1,0:T(1,128)} %param.6) | copy-start | bytes 1572868
  137.9 122.3 %all-gather.8.cloned.1.call-start = ((), (), s32[]{:S(2)}) async-start(), calls=%async_computation.8 | async-start | bytes 1081344 | tf_op jit(solution)/shard_map/all_gather | solution.py:91
  138.4 220.4 %reduce-scatter.11.cloned.1.call-start = ((), (), s32[]{:S(2)}) async-start(), calls=%async_computation.7 | async-start | bytes 540672 | tf_op jit(solution)/shard_map/reduce_scatter | solution.py:52
  250.8 5.5 copy-start.24
  253.6 213.1 %reduce-scatter.9.cloned.1.call-start = ((), (), s32[]{:S(2)}) async-start(), calls=%async_computation.6 | async-start | bytes 540672 | tf_op jit(solution)/shard_map/reduce_scatter | solution.py:52
  253.7 4.5 copy-start.27
  254.3 3.9 copy-start.26
  254.4 3.9 copy-start.23
  255.5 287.2 %all-gather.10.cloned.1.call-start = ((), (), s32[]{:S(2)}) async-start(), calls=%async_computation.9 | async-start | bytes 2703360 | tf_op jit(solution)/shard_map/all_gather | solution.py:89
  256.3 390.4 %reduce-scatter.7.cloned.1.call-start = ((), (), s32[]{:S(2)}) async-start(), calls=%async_computation.5 | async-start | bytes 540672 | tf_op jit(solution)/shard_map/reduce_scatter | solution.py:52
  258.1 496.7 %reduce-scatter.5.cloned.1.call-start = ((), (), s32[]{:S(2)}) async-start(), calls=%async_computation.4 | async-start | bytes 540672 | tf_op jit(solution)/shard_map/reduce_scatter | solution.py:52
  260.1 625.5 %all-reduce.9.cloned.1.call-start = ((), (), s32[]{:S(2)}) async-start(), calls=%async_computation.12 | async-start | bytes 5242880 | tf_op jit(solution)/shard_map/psum | solution.py:137
  542.7 212.1 %copy-start = (f32[10,256,256]{2,1,0:T(8,128)S(1)}, f32[10,256,256]{2,1,0:T(8,128)}, u32[]{:S(2)}) copy-start(f32[10,256,256]{2,1,0:T(8,128)} %all-gather.10.cloned.1.call-done) | copy-start | bytes 7864324
  761.5 124.9 %all-gather.12.cloned.1.call-start = ((), (), s32[]{:S(2)}) async-start(), calls=%async_computation.10 | async-start | bytes 2703360 | tf_op jit(solution)/shard_map/all_gather | solution.py:90
  762.1 339.9 %all-reduce.7.cloned.1.call-start = ((), (), s32[]{:S(2)}) async-start(), calls=%async_computation.11 | async-start | bytes 5242880 | tf_op jit(solution)/shard_map/psum | solution.py:137
  1106.5 5.0 copy-start.1
  1113.4 3.3 copy-start.11
  1113.4 5.4 copy-start.2
  1114.9 5.0 copy-start.20
  1116.7 5.4 copy-start.7
  1126.2 3.1 copy-start.8
  1126.2 3.9 copy-start.3
  1126.2 4.3 copy-start.5
  1130.5 7.0 copy-start.14
  1131.7 3.5 copy-start.22
  1132.1 4.7 copy-start.17
  1135.2 3.9 copy-start.13
  1138.6 3.3 copy-start.18
  1138.6 3.3 copy-start.6
  1138.6 3.3 copy-start.12
  1139.0 3.0 copy-start.15
  (6 other events, 13.3 us)
Sparse Core Ops, SparseCore 0:
  138.0 112.7 all-reduce.10
  761.6 123.9 all-reduce.8
Sparse Core Ops, SparseCore 1:
  140.5 67.5 all-gather.7
  253.7 105.0 reduce-scatter.10
  361.7 104.9 reduce-scatter.8
  468.8 73.8 all-gather.9
  545.5 101.1 reduce-scatter.6
  649.7 105.1 reduce-scatter.4
  764.1 73.4 all-gather.11
  885.7 216.2 all-reduce.6
